TPU v7x, 512 devices: a whole 4x4x16 slice. The times are simulated.
512 devices in a mesh: chan: 32 (over z_lo, y, core), day: 16 (over x, z_hi).
Axes of the slice: x: 4, y: 4, z: 16 (z_hi: 4, z_lo: 4; z = z_hi * 4 + z_lo), core: 2. Of those that a mesh axis runs over, the one named last changes fastest.
Arguments:
- records: bfloat16 [16, 2048, 4096], P('day', 'chan'), may hold values from -50 to 50
- filter_taps: bfloat16 [64], replicated, may hold values from -0.75 to 0.75
- window_offsets: int32 [16, 2], P('day'), may hold values from 0 to 3009, as said below
- pair_masks: int32 [3], replicated, may hold values from 1 to 31, as said below
Outputs:
- stacks: float32 [3, 65, 131072], P(None, None, ('chan', 'day'))
Inputs may be any that keep to these rules, and one draw needn't show every extreme that they name: `window_offsets`: in each day group one window ends at the record's last sample. `pair_masks`: the masks are distinct; 1 and 31 are among them.
All inputs are finite; a program needn't handle non-finite values.
Results may differ from a plain program's by a relative error of at most 0.0029.
Values may be sent and summed in bfloat16 or wider, within the bound.
A program may use at most 64 MiB of HBM per device.

v0:
```python
import functools

import jax
import jax.numpy as jnp
from jax import lax
from jax.experimental import pallas as pl
from jax.experimental.pallas import tpu as pltpu
from jax.sharding import PartitionSpec as P

MESH = pl.DeviceIdType.MESH
F32, BF16 = jnp.float32, jnp.bfloat16
NT = (((1,), (1,)), ((), ()))

L, MAXLAG, TAPS = 1024, 32, 64
LAGS = 2 * MAXLAG + 1
CH = 64
STEP = 16
DELAYS = STEP + 1
GAP = 128
ROW = 2 * (L + GAP)
RING = 4
XR = DELAYS * STEP
ZR = 4 * STEP
PART = 64
SPLIT = CH // PART
CHUNKS = 3 * SPLIT
WIDE = 4 * PART
X_MERGED = (0, 1)
Z_MERGED = (0, 1)
ORDER = ("C1", "M0", "M1", "X0", "C2", "X1", "N0", "N1", "X2", "Z0", "Z1", "Z2")
LAST = f"X{CHUNKS - 1}"


def whiten_kernel(offsets, record, taps, white, band):
    width = 384
    band[...] = jnp.zeros_like(band)
    band[0:1, 0:TAPS] = taps[...].astype(F32)
    rows = jnp.broadcast_to(band[0:1, :], (256, width))
    toeplitz = pltpu.roll(rows, 0, 1, stride=1, stride_axis=0).astype(BF16)
    span = 1280
    last = (record.shape[1] - span) // 128
    for w in range(2):
        start = offsets[0, w]
        tile = jnp.minimum(start // 128, last)
        base = pl.multiple_of(tile * 128, 128)
        data = record[:, pl.ds(base, span)].astype(F32)
        data = pltpu.roll(data, span - (start - base), 1).astype(BF16)
        parts = jnp.concatenate([data[:, 256 * m : 256 * m + width] for m in range(4)], axis=0)
        total = lax.dot_general(parts, toeplitz, NT, preferred_element_type=F32)
        square = jnp.sum(total * total, axis=1, keepdims=True)
        power = sum(square[CH * m : CH * (m + 1)] for m in range(4)) / L
        scale = lax.rsqrt(power + 1e-06)
        for m in range(4):
            lanes = slice(L * w + 256 * m, L * w + 256 * (m + 1))
            white[:, lanes] = (total[CH * m : CH * (m + 1)] * scale).astype(BF16)


def gapped(block):
    zeros = jnp.zeros((block.shape[0], GAP), BF16)
    return jnp.concatenate([block[:, :L], zeros, block[:, L:], zeros], axis=1)


class Ring:
    def __init__(self, right, left, far, to_r, to_l, to_f, hop_r, hop_l, got_r, got_l, got_f, send, recv):
        self.right, self.left, self.far = right, left, far
        self.to_r, self.to_l, self.to_f, self.hop_r, self.hop_l = to_r, to_l, to_f, hop_r, hop_l
        self.got_r, self.got_l, self.got_f = got_r, got_l, got_f
        self.send, self.recv = send, recv
        self.half = to_r.shape[1] // 2 // 16 * 16

    def copy(self, c, k, merged):
        if merged:
            lo, hi = pl.ds(0, self.half), pl.ds(self.half, self.to_r.shape[1] - self.half)
            src, dst, to = (
                (self.to_f.at[c, lo], self.hop_r.at[c], self.right),
                (self.to_f.at[c, hi], self.hop_l.at[c], self.left),
                (self.to_r.at[c, hi], self.got_l.at[c, hi], self.right),
                (self.to_l.at[c, lo], self.got_r.at[c, lo], self.left),
                (self.to_r.at[c, lo], self.got_l.at[c, lo], self.right),
                (self.to_l.at[c, hi], self.got_r.at[c, hi], self.left),
            )[k]
        else:
            src, dst, to = (
                (self.to_f.at[c], self.got_f.at[c], self.far),
                (self.to_r.at[c], self.got_l.at[c], self.right),
                (self.to_l.at[c], self.got_r.at[c], self.left),
            )[k]
        return pltpu.make_async_remote_copy(
            src_ref=src, dst_ref=dst, send_sem=self.send.at[c, k], recv_sem=self.recv.at[c, k],
            device_id={"day": to}, device_id_type=MESH,
        )


def reduce_kernel(
    own, middle, near, out,
    astack, bstack, distant, c_own, c_r, c_l, s_buf, z_buf, t_buf, e_own, e_send, e_got,
    x_r, x_l, x_f, x_hr, x_hl, x_gr, x_gl, x_gf, xs, xd,
    z_r, z_l, z_f, z_hr, z_hl, z_gr, z_gl, z_gf, zs, zd,
    es, ed, ps, pd,
):
    day, chan = lax.axis_index("day"), lax.axis_index("chan")
    x, zh = day // RING, day % RING
    x_to = [((x + k) % RING) * RING + zh for k in range(RING)]
    z_to = [x * RING + (zh + k) % RING for k in range(RING)]
    far_to = lax.axis_size("chan") - 1 - chan
    barrier = pltpu.get_barrier_semaphore()
    for other in (*x_to[1:], *z_to[1:]):
        pl.semaphore_signal(barrier, inc=1, device_id={"day": other}, device_id_type=MESH)
    pl.semaphore_signal(barrier, inc=1, device_id={"chan": far_to}, device_id_type=MESH)

    xring = Ring(x_to[1], x_to[3], x_to[2], x_r, x_l, x_f, x_hr, x_hl, x_gr, x_gl, x_gf, xs, xd)
    zring = Ring(z_to[1], z_to[3], z_to[2], z_r, z_l, z_f, z_hr, z_hl, z_gr, z_gl, z_gf, zs, zd)

    def block_copy(h):
        rows = pl.ds(PART * h, PART)
        return pltpu.make_async_remote_copy(
            src_ref=own.at[rows], dst_ref=distant.at[rows], send_sem=ps.at[h], recv_sem=pd.at[h],
            device_id={"chan": far_to}, device_id_type=MESH,
        )

    mine = gapped(own[...])
    for a in range(DELAYS):
        moved = pltpu.roll(mine, a, 1) if a else mine
        for part in range(RING):
            astack[part, 16 * a : 16 * a + 16, :] = moved[16 * part : 16 * part + 16]

    norm = 1.0 / jnp.sqrt(jnp.float32(16 * 2 * L))

    def product(k):
        return lax.dot_general(astack[(x + k) % RING], bstack[...], NT, preferred_element_type=F32)

    def compute(c, start=True):
        r, h = c // SPLIT, c % SPLIT
        merged, half = c in X_MERGED, xring.half
        if r == 2:
            block_copy(h).wait_recv()
        theirs = gapped((middle, near, distant)[r][PART * h : PART * (h + 1)])
        for b in range(4):
            shift = (MAXLAG - STEP * b) % ROW
            bstack[PART * b : PART * (b + 1), :] = pltpu.roll(theirs, shift, 1) if shift else theirs
        x_f[c] = product(2).astype(BF16)
        if start:
            x_start(c, (0, 1) if merged else (0,))
        piece = product(1)
        if merged:
            x_r[c, half:] = piece[half:].astype(BF16)
            c_r[c] = piece[:half]
        else:
            x_r[c] = piece.astype(BF16)
        if start:
            x_start(c, (2,) if merged else (1,))
        piece = product(3)
        if merged:
            x_l[c, :half] = piece[:half].astype(BF16)
            c_l[c] = piece[half:]
        else:
            x_l[c] = piece.astype(BF16)
        if start:
            x_start(c, (3,) if merged else (2,))
        c_own[c] = product(0)

    def x_start(c, which):
        for k in which:
            xring.copy(c, k, c in X_MERGED).start()

    def x_merge(c):
        half = xring.half
        xring.copy(c, 0, True).wait_recv()
        x_r[c, :half] = (c_r[c] + x_hr[c].astype(F32)).astype(BF16)
        xring.copy(c, 4, True).start()
        xring.copy(c, 1, True).wait_recv()
        x_l[c, half:] = (c_l[c] + x_hl[c].astype(F32)).astype(BF16)
        xring.copy(c, 5, True).start()

    def x_end(c):
        merged = c in X_MERGED
        for k in range(2, 6) if merged else range(3):
            xring.copy(c, k, merged).wait_recv()
        total = c_own[c] + x_gl[c].astype(F32) + x_gr[c].astype(F32)
        if not merged:
            total += x_gf[c].astype(F32)
        for side in range(WIDE // 128):
            lanes = slice(128 * side, 128 * (side + 1))
            s_buf[side] = total[:, lanes]
            for part in range(RING):
                for i in range(4):
                    z_buf[c, part, 16 * i : 16 * i + 16, lanes] = s_buf[side, pl.ds(4 * part + i, 16, stride=16), :]
        e_own[:, PART * c : PART * (c + 1)] = total[256:272, 3 * PART :]
        merged = c in Z_MERGED
        z_f[c] = z_buf[c, (zh + 2) % RING].astype(BF16)
        if not merged:
            zring.copy(c, 0, merged).start()
            z_r[c] = z_buf[c, (zh + 1) % RING].astype(BF16)
            zring.copy(c, 1, merged).start()
            z_l[c] = z_buf[c, (zh + 3) % RING].astype(BF16)
            zring.copy(c, 2, merged).start()
        else:
            zring.copy(c, 0, merged).start()
            zring.copy(c, 1, merged).start()
            half = zring.half
            z_r[c, half:] = z_buf[c, (zh + 1) % RING, half:].astype(BF16)
            zring.copy(c, 2, merged).start()
            z_l[c, :half] = z_buf[c, (zh + 3) % RING, :half].astype(BF16)
            zring.copy(c, 3, merged).start()

    def z_merge(c):
        half = zring.half
        zring.copy(c, 0, True).wait_recv()
        z_r[c, :half] = (z_buf[c, (zh + 1) % RING, :half] + z_hr[c].astype(F32)).astype(BF16)
        zring.copy(c, 4, True).start()
        zring.copy(c, 1, True).wait_recv()
        z_l[c, half:] = (z_buf[c, (zh + 3) % RING, half:] + z_hl[c].astype(F32)).astype(BF16)
        zring.copy(c, 5, True).start()

    def z_end(c):
        merged = c in Z_MERGED
        for k in range(2, 6) if merged else range(3):
            zring.copy(c, k, merged).wait_recv()
        total = z_buf[c, zh] + z_gl[c].astype(F32) + z_gr[c].astype(F32)
        if not merged:
            total += z_gf[c].astype(F32)
        t_buf[c] = total * norm
        if c % SPLIT == SPLIT - 1:
            first = c + 1 - SPLIT
            for b in range(4):
                cut = [t_buf[first + h, :, PART * b : PART * (b + 1)] for h in range(SPLIT)]
                out[c // SPLIT, 16 * b : 16 * b + 16, :] = jnp.concatenate(
                    [cut[h][16 * i : 16 * i + 16] for i in range(4) for h in range(SPLIT)], axis=1
                )

    def e_copy(k):
        return pltpu.make_async_remote_copy(
            src_ref=e_send, dst_ref=e_got.at[k - 1], send_sem=es.at[k - 1], recv_sem=ed.at[k - 1],
            device_id={"day": z_to[k]}, device_id_type=MESH,
        )

    steps = {"C": compute, "M": x_merge, "X": x_end, "N": z_merge, "Z": z_end}
    compute(0, start=False)
    pl.semaphore_wait(barrier, 7)
    for h in range(SPLIT):
        block_copy(h).start()
    x_start(0, range(4) if 0 in X_MERGED else range(3))
    for step in ORDER:
        steps[step[0]](int(step[1:]))
        if step == LAST:
            e_send[...] = e_own[...].astype(BF16)
            for k in range(1, RING):
                e_copy(k).start()

    for k in range(1, RING):
        e_copy(k).wait_recv()
    tails = (e_own[...] + sum(e_got[k].astype(F32) for k in range(3))) * norm
    tail = tails[0:4]
    for part in range(1, RING):
        tail = jnp.where(zh == part, tails[4 * part : 4 * part + 4], tail)
    for r in range(3):
        out[r, 64:65, :] = jnp.concatenate([tail[i : i + 1, CH * r : CH * (r + 1)] for i in range(4)], axis=1)

    for k in range(1, RING):
        e_copy(k).wait_send()
    for h in range(SPLIT):
        block_copy(h).wait_send()
    for c in range(CHUNKS):
        for k in range(6 if c in X_MERGED else 3):
            xring.copy(c, k, c in X_MERGED).wait_send()
        for k in range(6 if c in Z_MERGED else 3):
            zring.copy(c, k, c in Z_MERGED).wait_send()


def exchange_kernel(mask, own, middle, near, send, recv):
    chan, count = lax.axis_index("chan"), lax.axis_size("chan")
    flip = sum((1 - 2 * (chan // 2**k % 2)) * 2**k for k in range(count.bit_length() - 1) if mask >> k & 1)
    to = (chan + flip, chan + 1 - 2 * (chan % 2))
    barrier = pltpu.get_barrier_semaphore()
    for other in to:
        pl.semaphore_signal(barrier, inc=1, device_id={"chan": other}, device_id_type=MESH)
    pl.semaphore_wait(barrier, 2)
    copies = [
        pltpu.make_async_remote_copy(
            src_ref=own, dst_ref=dst, send_sem=send.at[k], recv_sem=recv.at[k],
            device_id={"chan": to[k]}, device_id_type=MESH,
        )
        for k, dst in enumerate((middle, near))
    ]
    for copy in copies:
        copy.start()
    for copy in copies:
        copy.wait()


def exchange(white, mask):
    vmem = pl.BlockSpec(memory_space=pltpu.VMEM)
    shape = jax.ShapeDtypeStruct(white.shape, white.dtype)
    return pl.pallas_call(
        functools.partial(exchange_kernel, mask),
        out_shape=(shape,) * 2,
        in_specs=[vmem],
        out_specs=(vmem,) * 2,
        scratch_shapes=[pltpu.SemaphoreType.DMA((2,)), pltpu.SemaphoreType.DMA((2,))],
        compiler_params=pltpu.CompilerParams(collective_id=mask, has_side_effects=True, vmem_limit_bytes=8 << 20),
        name=f"exchange{mask}",
    )(white)


def correlate(white, other, near):
    def chunks(rows, kind=BF16):
        return pltpu.VMEM((CHUNKS, rows, WIDE), kind)

    def sems(*shape):
        return pltpu.SemaphoreType.DMA(shape)

    vmem = pl.BlockSpec(memory_space=pltpu.VMEM)
    return pl.pallas_call(
        reduce_kernel,
        out_shape=jax.ShapeDtypeStruct((3, LAGS, 256), F32),
        in_specs=[vmem] * 3,
        out_specs=vmem,
        scratch_shapes=[
            pltpu.VMEM((RING, XR, ROW), BF16),
            pltpu.VMEM((WIDE, ROW), BF16),
            pltpu.VMEM((CH, 2 * L), BF16),
            chunks(XR, F32),
            chunks(XR // 32 * 16, F32),
            chunks(XR - XR // 32 * 16, F32),
            pltpu.VMEM((WIDE // 128, XR, 128), F32),
            pltpu.VMEM((CHUNKS, RING, ZR, WIDE), F32),
            chunks(ZR, F32),
            pltpu.VMEM((16, CHUNKS * PART), F32),
            pltpu.VMEM((16, CHUNKS * PART), BF16),
            pltpu.VMEM((3, 16, CHUNKS * PART), BF16),
            *[chunks(XR) for _ in range(3)],
            chunks(XR // 32 * 16),
            chunks(XR - XR // 32 * 16),
            *[chunks(XR) for _ in range(3)],
            sems(CHUNKS, 6), sems(CHUNKS, 6),
            *[chunks(ZR) for _ in range(3)],
            *[chunks(ZR // 2) for _ in range(2)],
            *[chunks(ZR) for _ in range(3)],
            sems(CHUNKS, 6), sems(CHUNKS, 6),
            sems(3), sems(3),
            sems(SPLIT), sems(SPLIT),
        ],
        compiler_params=pltpu.CompilerParams(collective_id=0, has_side_effects=True, vmem_limit_bytes=48 << 20),
        name="correlate",
    )(white, other, near)


def local(records, filter_taps, window_offsets, pair_masks):
    count = lax.axis_size("chan")
    middle = jnp.sum(pair_masks) - count
    vmem = pl.BlockSpec(memory_space=pltpu.VMEM)
    white = pl.pallas_call(
        whiten_kernel,
        out_shape=jax.ShapeDtypeStruct((CH, 2 * L), BF16),
        in_specs=[pl.BlockSpec(memory_space=pltpu.SMEM), vmem, vmem],
        out_specs=vmem,
        scratch_shapes=[pltpu.VMEM((8, 384), F32)],
        compiler_params=pltpu.CompilerParams(vmem_limit_bytes=16 << 20),
        name="whiten",
    )(window_offsets, records[0], filter_taps[None])

    branches = [functools.partial(exchange, mask=m) for m in range(2, count - 1)]
    other, near = lax.switch(middle - 2, branches, white)
    res = correlate(white, other, near)
    kind = pair_masks[:, None, None]
    return jnp.where(kind == 1, res[1], jnp.where(kind == count - 1, res[2], res[0]))


def solution(mesh):
    in_specs = (P("day", "chan", None), P(), P("day", None), P())
    out_specs = P(None, None, ("chan", "day"))
    return jax.shard_map(local, mesh=mesh, in_specs=in_specs, out_specs=out_specs, check_vma=False)
```

profile of v0, /device:TPU:68, one launch (start us, length us, event | category | flops | bytes accessed | tf_op | source)
XLA Modules:
  0.0 69.0 jit_solution(1660995050337649487)
XLA Ops:
  0.0 0.0 copy-start.1
  0.0 0.0 copy-start.2
  0.0 0.7 copy-done.1
  0.7 0.0 copy-done.2
  0.7 0.0 copy-start
  0.7 1.0 %copy-done = bf16[1,64,4096]{2,1,0:T(8,128)(2,1)S(1)} copy-done((bf16[1,64,4096]{2,1,0:T(8,128)(2,1)S(1)}, bf16[1,64,4096]{2,1,0:T(8,128)(2,1)}, u32[]{:S(2)}) %copy-start) | copy-done | bytes 524312
  1.7 0.0 copy-start.3
  1.7 1.1 %whiten.1.own = bf16[64,2048]{1,0:T(8,128)(2,1)S(1)} custom-call(s32[1,2]{1,0:T(1,128)S(1)} %copy-done.1, bf16[64,4096]{1,0:T(8,128)(2,1)S(1)} %bitcast.8, bf16[1,64]{1,0:T(2,128)(2,1)S(1)} %bitcast.9), custom_call_target="tpu_custom_call" | custom-call | tf_op jit(solution)/shard_map/whiten/pallas_call | solution.py:352
  2.8 0.0 copy-done.3
  2.8 0.6 reduce_sum.9
  4.1 16.9 %conditional.1 = ((bf16[64,2048]{1,0:T(8,128)(2,1)S(1)}, bf16[64,2048]{1,0:T(8,128)(2,1)S(1)})) conditional(s32[]{:T(128)} %clamp.3, bf16[64,2048]{1,0:T(8,128)(2,1)S(1)} %whiten.1.own, bf16[64,2048]{1,0:T(8,128)(2,1)S(1)} %whiten.1.own, bf16[64,2048]{1,0:T(8,128)(2,1)S(1)} %whiten.1.own, ...), branch_computations={%region_1.0_spmd, %region_2.0_spmd, %region_3.0_spmd, %region_4.0_... | conditional | bytes 8 | solution.py:363
  4.2 16.8 %exchange28.1 = (bf16[64,2048]{1,0:T(8,128)(2,1)S(1)}, bf16[64,2048]{1,0:T(8,128)(2,1)S(1)}) custom-call(bf16[64,2048]{1,0:T(8,128)(2,1)S(1)} %own.26), custom_call_target="tpu_custom_call" | custom-call | tf_op jit(solution)/shard_map/cond/branch_26_fun/exchange28/pallas_call | solution.py:294
  21.0 47.2 %correlate.1 = f32[3,65,256]{2,1,0:T(8,128)S(1)} custom-call(bf16[64,2048]{1,0:T(8,128)(2,1)S(1)} %whiten.1.own, bf16[64,2048]{1,0:T(8,128)(2,1)S(1)} %get-tuple-element.36.middle, bf16[64,2048]{1,0:T(8,128)(2,1)S(1)} %get-tuple-element.37.near), custom_call_target="tpu_custom_call" | custom-call | tf_op jit(solution)/shard_map/correlate/pallas_call | solution.py:313
  68.2 0.8 %select_select_fusion = f32[3,65,256]{2,1,0:T(8,128)} fusion(f32[65,256]{1,0:T(8,128)S(1)} %get-tuple-element.39, f32[65,256]{1,0:T(8,128)S(1)} %get-tuple-element.40, f32[65,256]{1,0:T(8,128)S(1)} %get-tuple-element.38, pred[3]{0:T(512)(128)(4,1)S(1)} %get-tuple-element.42, pred[3]{0:T(512)(128)(4,1)S(1)} %get-tuple-element.41), kind=kLoop, calls=%fused_computation | loop fusion | flops 99840 | bytes 399366 | tf_op jit(solution)/shard_map/jit(_where)/select_n | solution.py:366
  (2 shorter events, 0.0 us)
Async XLA Ops:
  0.0 0.7 copy-start.1
  0.0 0.7 copy-start.2
  0.7 1.0 %copy-start = (bf16[1,64,4096]{2,1,0:T(8,128)(2,1)S(1)}, bf16[1,64,4096]{2,1,0:T(8,128)(2,1)}, u32[]{:S(2)}) copy-start(bf16[1,64,4096]{2,1,0:T(8,128)(2,1)} %param.33) | copy-start | bytes 1572868
  1.7 1.1 %copy-start.3 = (s32[3]{0:T(128)S(1)}, s32[3]{0:T(128)}, u32[]{:S(2)}) copy-start(s32[3]{0:T(128)} %param.36) | copy-start | bytes 40
where the time goes:
time: 69.2 us; the launch traced here: 69 us
  Pallas kernels  65.1 us (94%)
  local copies, waits for them, and re-layouts  1.73 us (2%)
  other arithmetic  1.42 us (2%)
  between operations  0.71 us (1%)
    pallas_call x1, Pallas kernels, correlate(): pl.pallas_call(reduce_kernel, out_shape=jax.ShapeDtypeStruct((3, LAGS, 25...  47.2 us
    pallas_call x1, Pallas kernels, exchange(): pl.pallas_call(functools.partial(exchange_kernel, mask), out_shape=(shape...  16.8 us
    unnamed x8, local copies, waits for them, and re-layouts  1.71 us

commit v1 on v0

--- a/solution.py
+++ b/solution.py
@@ -69,8 +69,8 @@
         self.half = to_r.shape[1] // 2 // 16 * 16
 
     def copy(self, c, k, merged):
+        lo, hi = pl.ds(0, self.half), pl.ds(self.half, self.to_r.shape[1] - self.half)
         if merged:
-            lo, hi = pl.ds(0, self.half), pl.ds(self.half, self.to_r.shape[1] - self.half)
             src, dst, to = (
                 (self.to_f.at[c, lo], self.hop_r.at[c], self.right),
                 (self.to_f.at[c, hi], self.hop_l.at[c], self.left),
@@ -80,11 +80,13 @@
                 (self.to_l.at[c, hi], self.got_r.at[c, hi], self.left),
             )[k]
         else:
+            rows = (lo, hi)[k // 3]
             src, dst, to = (
-                (self.to_f.at[c], self.got_f.at[c], self.far),
-                (self.to_r.at[c], self.got_l.at[c], self.right),
-                (self.to_l.at[c], self.got_r.at[c], self.left),
-            )[k]
+                (self.to_f, self.got_f, self.far),
+                (self.to_r, self.got_l, self.right),
+                (self.to_l, self.got_r, self.left),
+            )[k % 3]
+            src, dst = src.at[c, rows], dst.at[c, rows]
         return pltpu.make_async_remote_copy(
             src_ref=src, dst_ref=dst, send_sem=self.send.at[c, k], recv_sem=self.recv.at[c, k],
             device_id={"day": to}, device_id_type=MESH,
@@ -156,7 +158,7 @@
         else:
             x_l[c] = piece.astype(BF16)
         if start:
-            x_start(c, (3,) if merged else (2,))
+            x_start(c, (3,) if merged else (2, 3, 4, 5))
         c_own[c] = product(0)
 
     def x_start(c, which):
@@ -172,8 +174,31 @@
         x_l[c, half:] = (c_l[c] + x_hl[c].astype(F32)).astype(BF16)
         xring.copy(c, 5, True).start()
 
+    def x_halves(c):
+        for g in range(2):
+            for k in range(3 * g, 3 * g + 3):
+                xring.copy(c, k, False).wait_recv()
+            rows = slice(0, xring.half) if g == 0 else slice(xring.half, XR)
+            total = c_own[c, rows] + x_gl[c, rows].astype(F32) + x_gr[c, rows].astype(F32) + x_gf[c, rows].astype(F32)
+            for side in range(WIDE // 128):
+                lanes = slice(128 * side, 128 * (side + 1))
+                s_buf[side, rows] = total[:, lanes]
+                for part in range(RING):
+                    for i in range(4):
+                        z_buf[c, part, 32 * g + 8 * i : 32 * g + 8 * i + 8, lanes] = s_buf[
+                            side, pl.ds(128 * g + 4 * part + i, 8, stride=16), :
+                        ]
+            half = pl.ds(32 * g, 32)
+            for k, ref, off in ((0, z_f, 2), (1, z_r, 1), (2, z_l, 3)):
+                ref[c, half] = z_buf[c, (zh + off) % RING, half].astype(BF16)
+                zring.copy(c, 3 * g + k, False).start()
+            if g:
+                e_own[:, PART * c : PART * (c + 1)] = total[128:144, 3 * PART :]
+
     def x_end(c):
         merged = c in X_MERGED
+        if not merged:
+            return x_halves(c)
         for k in range(2, 6) if merged else range(3):
             xring.copy(c, k, merged).wait_recv()
         total = c_own[c] + x_gl[c].astype(F32) + x_gr[c].astype(F32)
@@ -214,12 +239,17 @@
 
     def z_end(c):
         merged = c in Z_MERGED
-        for k in range(2, 6) if merged else range(3):
+        for k in range(2, 6) if merged else range(6):
             zring.copy(c, k, merged).wait_recv()
         total = z_buf[c, zh] + z_gl[c].astype(F32) + z_gr[c].astype(F32)
         if not merged:
             total += z_gf[c].astype(F32)
-        t_buf[c] = total * norm
+        if merged:
+            t_buf[c] = total * norm
+        else:
+            for g in range(2):
+                for i in range(4):
+                    t_buf[c, 16 * i + 8 * g : 16 * i + 8 * g + 8] = total[32 * g + 8 * i : 32 * g + 8 * i + 8] * norm
         if c % SPLIT == SPLIT - 1:
             first = c + 1 - SPLIT
             for b in range(4):
@@ -261,9 +291,9 @@
     for h in range(SPLIT):
         block_copy(h).wait_send()
     for c in range(CHUNKS):
-        for k in range(6 if c in X_MERGED else 3):
+        for k in range(6):
             xring.copy(c, k, c in X_MERGED).wait_send()
-        for k in range(6 if c in Z_MERGED else 3):
+        for k in range(6):
             zring.copy(c, k, c in Z_MERGED).wait_send()
 
 

time: 69.2 us -> 69.7 us (level)
  the two profiles are of different devices: /device:TPU:68 before, /device:TPU:38 now
where the time goes in v1:
time: 69.7 us; the launch traced here: 69.2 us
  Pallas kernels  65.3 us (94%)
  local copies, waits for them, and re-layouts  1.73 us (2%)
  other arithmetic  1.42 us (2%)
  between operations  0.71 us (1%)
    pallas_call x1, Pallas kernels, correlate(): pl.pallas_call(reduce_kernel, out_shape=jax.ShapeDtypeStruct((3, LAGS, 25...  47.9 us
    pallas_call x1, Pallas kernels, exchange(): pl.pallas_call(functools.partial(exchange_kernel, mask), out_shape=(shape...  16.3 us
    unnamed x8, local copies, waits for them, and re-layouts  1.71 us

profile of v1, /device:TPU:38, one launch (start us, length us, event | category | flops | bytes accessed | tf_op | source)
XLA Modules:
  0.0 69.2 jit_solution(166292567108306470)
XLA Ops:
  0.0 0.0 copy-start.1
  0.0 0.0 copy-start.2
  0.0 0.7 copy-done.1
  0.7 0.0 copy-done.2
  0.7 0.0 copy-start
  0.7 1.0 %copy-done = bf16[1,64,4096]{2,1,0:T(8,128)(2,1)S(1)} copy-done((bf16[1,64,4096]{2,1,0:T(8,128)(2,1)S(1)}, bf16[1,64,4096]{2,1,0:T(8,128)(2,1)}, u32[]{:S(2)}) %copy-start) | copy-done | bytes 524312
  1.7 0.0 copy-start.3
  1.7 1.1 %whiten.1.own = bf16[64,2048]{1,0:T(8,128)(2,1)S(1)} custom-call(s32[1,2]{1,0:T(1,128)S(1)} %copy-done.1, bf16[64,4096]{1,0:T(8,128)(2,1)S(1)} %bitcast.8, bf16[1,64]{1,0:T(2,128)(2,1)S(1)} %bitcast.9), custom_call_target="tpu_custom_call" | custom-call | tf_op jit(solution)/shard_map/whiten/pallas_call | solution.py:382
  2.8 0.0 copy-done.3
  2.8 0.6 reduce_sum.9
  4.1 16.4 %conditional.1 = ((bf16[64,2048]{1,0:T(8,128)(2,1)S(1)}, bf16[64,2048]{1,0:T(8,128)(2,1)S(1)})) conditional(s32[]{:T(128)} %clamp.3, bf16[64,2048]{1,0:T(8,128)(2,1)S(1)} %whiten.1.own, bf16[64,2048]{1,0:T(8,128)(2,1)S(1)} %whiten.1.own, bf16[64,2048]{1,0:T(8,128)(2,1)S(1)} %whiten.1.own, ...), branch_computations={%region_1.0_spmd, %region_2.0_spmd, %region_3.0_spmd, %region_4.0_... | conditional | bytes 8 | solution.py:393
  4.2 16.3 %exchange19.1 = (bf16[64,2048]{1,0:T(8,128)(2,1)S(1)}, bf16[64,2048]{1,0:T(8,128)(2,1)S(1)}) custom-call(bf16[64,2048]{1,0:T(8,128)(2,1)S(1)} %own.17), custom_call_target="tpu_custom_call" | custom-call | tf_op jit(solution)/shard_map/cond/branch_17_fun/exchange19/pallas_call | solution.py:324
  20.5 47.9 %correlate.1 = f32[3,65,256]{2,1,0:T(8,128)S(1)} custom-call(bf16[64,2048]{1,0:T(8,128)(2,1)S(1)} %whiten.1.own, bf16[64,2048]{1,0:T(8,128)(2,1)S(1)} %get-tuple-element.36.middle, bf16[64,2048]{1,0:T(8,128)(2,1)S(1)} %get-tuple-element.37.near), custom_call_target="tpu_custom_call" | custom-call | tf_op jit(solution)/shard_map/correlate/pallas_call | solution.py:343
  68.4 0.8 %select_select_fusion = f32[3,65,256]{2,1,0:T(8,128)} fusion(f32[65,256]{1,0:T(8,128)S(1)} %get-tuple-element.39, f32[65,256]{1,0:T(8,128)S(1)} %get-tuple-element.40, f32[65,256]{1,0:T(8,128)S(1)} %get-tuple-element.38, pred[3]{0:T(512)(128)(4,1)S(1)} %get-tuple-element.42, pred[3]{0:T(512)(128)(4,1)S(1)} %get-tuple-element.41), kind=kLoop, calls=%fused_computation | loop fusion | flops 99840 | bytes 399366 | tf_op jit(solution)/shard_map/jit(_where)/select_n | solution.py:396
  (2 shorter events, 0.0 us)
Async XLA Ops:
  0.0 0.7 copy-start.1
  0.0 0.7 copy-start.2
  0.7 1.0 %copy-start = (bf16[1,64,4096]{2,1,0:T(8,128)(2,1)S(1)}, bf16[1,64,4096]{2,1,0:T(8,128)(2,1)}, u32[]{:S(2)}) copy-start(bf16[1,64,4096]{2,1,0:T(8,128)(2,1)} %param.33) | copy-start | bytes 1572868
  1.7 1.1 %copy-start.3 = (s32[3]{0:T(128)S(1)}, s32[3]{0:T(128)}, u32[]{:S(2)}) copy-start(s32[3]{0:T(128)} %param.36) | copy-start | bytes 40
